TPU v7x, 32 devices: a whole 2x2x4 slice. The times are simulated.
32 devices in a mesh: dp: 8 (over z, x), head: 4 (over y, core).
Axes of the slice: x: 2, y: 2, z: 4, core: 2. Of those that a mesh axis runs over, the one named last changes fastest.
Arguments:
- residual: bfloat16 [32, 4096], P('dp', 'head'), may hold values from -6 to 6
- query: bfloat16 [32, 32, 128], P('dp', 'head'), may hold values from -4.5 to 4.5
- fresh_token_keys: bfloat16 [32, 8, 128], P('dp', 'head'), may hold values from -4.5 to 4.5
- value_new: bfloat16 [32, 8, 128], P('dp', 'head'), may hold values from -24 to 24
- key_cache: bfloat16 [32, 8, 2048, 128], P('dp', 'head'), may hold values from -6 to 6
- value_cache: bfloat16 [32, 8, 2048, 128], P('dp', 'head'), may hold values from -6 to 6
- lengths: int32 [32], P('dp'), may hold values from 1024 to 2048, as said below
- pages: int32 [32, 8, 64], P('dp', 'head'), may hold values from 0 to 127, as said below
- w_out: bfloat16 [4096, 4096], P('head', 'dp'), may hold values from -0.75 to 0.75
- norm_gain: float32 [4096], P('head'), may hold values from 0.5 to 1.5
- expert_ids: int32 [32, 2], P('dp'), may hold values from 0 to 7, all different within a row; in each aligned block of 4 rows (0 to 3, 4 to 7, ...) at most 2 rows name the same one
- gate_weights: float32 [32, 2], P('dp'), may hold values from 0.1 to 1
- w_in: bfloat16 [8, 2, 4096, 7168], P('dp', None, None, 'head'), may hold values from -0.09375 to 0.09375
- w_down: bfloat16 [8, 7168, 4096], P('dp', 'head'), may hold values from -0.0625 to 0.0625
Outputs:
- layer_out: bfloat16 [32, 4096], P('dp', 'head')
Inputs may be any that keep to these rules, and one draw needn't show every extreme that they name: `lengths`: each request's length; some request has exactly 2048 and some exactly 1024. `pages`: for each request and key head, 64 distinct page numbers, all below ceil(length / 16), always including the page that holds the request's last cached token; in no fixed order. `expert_ids`: per token 2 distinct experts; among the 4 tokens of one dp index no expert is named more than 2 times.
All inputs are finite; a program needn't handle non-finite values.
Results may differ from a plain program's by a relative error of at most 0.012.
Values may be sent and summed in bfloat16 or wider, within the bound.
A program may use at most 128 MiB of HBM per device.

v0:
```python
import jax
import jax.numpy as jnp
from jax import lax
from jax.sharding import PartitionSpec as P

EXPERTS = 8
TOP = 2
PAGE = 16
MOST = 2
EPSILON = 1e-05


def shards(
    residual,
    query,
    fresh_token_keys,
    value_new,
    key_cache,
    value_cache,
    lengths,
    pages,
    w_out,
    norm_gain,
    expert_ids,
    gate_weights,
    w_in,
    w_down,
):
    tok_rows = query.shape[0]
    head_local = query.shape[1]
    head_dim = query.shape[2]
    kv_local = key_cache.shape[1]
    cache_len = key_cache.shape[2]
    page_total = cache_len // PAGE
    group_member_count = head_local // kv_local
    page_numbers = jnp.arange(page_total, dtype=jnp.int32)
    page_chosen = jnp.any(pages[:, :, :, None] == page_numbers[None, None, None, :], axis=2)
    position_chosen = jnp.broadcast_to(
        page_chosen[:, :, :, None], (tok_rows, kv_local, page_total, PAGE)
    ).reshape(tok_rows, kv_local, cache_len)
    position_ids = jnp.arange(cache_len, dtype=jnp.int32)
    in_range = (position_chosen & (position_ids[None, None, :] < lengths[:, None, None]))[
        :, :, None, :
    ]
    grouped_rows = query.reshape(tok_rows, kv_local, group_member_count, head_dim)
    score_scale = head_dim ** (-0.5)
    scores = (
        jnp.einsum("bkgd,bksd->bkgs", grouped_rows, key_cache, preferred_element_type=jnp.float32)
        * score_scale
    )
    own_score = (
        jnp.einsum(
            "luxe,lue->lux", grouped_rows, fresh_token_keys, preferred_element_type=jnp.float32
        )
        * score_scale
    )
    masked = jnp.where(in_range, scores, -1e30)
    row_top = jnp.maximum(jnp.max(masked, axis=-1), own_score)
    expo = jnp.where(in_range, jnp.exp(scores - row_top[..., None]), 0.0)
    own_expo = jnp.exp(own_score - row_top)
    denominator = jnp.sum(expo, axis=-1) + own_expo
    weights = (expo / denominator[..., None]).astype(jnp.bfloat16)
    own_weight = (own_expo / denominator).astype(jnp.bfloat16)
    attended = jnp.einsum(
        "bkgs,bksd->bkgd", weights, value_cache, preferred_element_type=jnp.float32
    )
    attended = (
        attended
        + own_weight.astype(jnp.float32)[..., None] * value_new.astype(jnp.float32)[:, :, None, :]
    )
    attn_rows = attended.reshape(tok_rows, head_local * head_dim).astype(jnp.bfloat16)
    every_row = lax.all_gather(attn_rows, "dp", axis=0, tiled=True)
    column_part = jnp.dot(every_row, w_out, preferred_element_type=jnp.float32)
    head_partial = lax.all_to_all(
        column_part.astype(jnp.bfloat16), "dp", split_axis=0, concat_axis=1, tiled=True
    ).astype(column_part.dtype)
    stream = residual.astype(jnp.float32) + lax.psum_scatter(
        head_partial.astype(jnp.bfloat16), "head", scatter_dimension=1, tiled=True
    ).astype(jnp.float32)
    whole_stream, whole_gain = (
        lax.all_gather(stream, "head", axis=1, tiled=True),
        lax.all_gather(norm_gain, "head", axis=0, tiled=True),
    )
    square_mean_value = jnp.mean(whole_stream * whole_stream, axis=-1)
    normed = (
        whole_stream * lax.rsqrt(square_mean_value + EPSILON)[:, None] * whole_gain[None, :]
    ).astype(jnp.bfloat16)
    group_count = lax.axis_size("dp") // EXPERTS
    assignments = tok_rows * TOP
    flat_ids = expert_ids.reshape(assignments)
    expert_range = jnp.arange(EXPERTS, dtype=jnp.int32)
    onehot = (flat_ids[:, None] == expert_range[None, :]).astype(jnp.int32)
    earlier = jnp.cumsum(onehot, axis=0) - onehot
    slot_index = jnp.sum(earlier * onehot, axis=1)
    target = flat_ids * MOST + slot_index
    placement_map = jnp.arange(EXPERTS * MOST, dtype=jnp.int32)[:, None] == target[None, :]
    token_map = jnp.any(placement_map.reshape(EXPERTS * MOST, tok_rows, TOP), axis=2)
    outgoing = jnp.dot(
        token_map.astype(jnp.bfloat16), normed, preferred_element_type=jnp.float32
    ).astype(jnp.bfloat16)
    width_of_row = outgoing.shape[1]
    outgoing = jnp.broadcast_to(
        outgoing.reshape(EXPERTS, 1, MOST, width_of_row), (EXPERTS, group_count, MOST, width_of_row)
    )
    outgoing = outgoing.reshape(EXPERTS * group_count, MOST, width_of_row)
    arrived = lax.all_to_all(outgoing, "dp", split_axis=0, concat_axis=0, tiled=True)
    senders, slot_count, feature_count = arrived.shape
    flat_rows = arrived.reshape(senders * slot_count, feature_count)
    gate_act = jnp.dot(flat_rows, w_in[0, 0], preferred_element_type=jnp.float32)
    up_act = jnp.dot(flat_rows, w_in[0, 1], preferred_element_type=jnp.float32)
    hidden = (jax.nn.silu(gate_act) * up_act).astype(jnp.bfloat16)
    slab_out = jnp.dot(hidden, w_down[0], preferred_element_type=jnp.float32).reshape(
        senders, slot_count, w_down.shape[2]
    )
    summed_total = lax.psum_scatter(
        slab_out.astype(jnp.bfloat16), "head", scatter_dimension=2, tiled=True
    ).astype(jnp.float32)
    returned = lax.all_to_all(
        summed_total.astype(jnp.bfloat16), "dp", split_axis=0, concat_axis=0, tiled=True
    ).astype(summed_total.dtype)
    local_width = returned.shape[2]
    per_expert = jnp.sum(returned.reshape(EXPERTS, group_count, MOST, local_width), axis=1).reshape(
        EXPERTS * MOST, local_width
    )
    weighted = jnp.where(placement_map, gate_weights.reshape(assignments)[None, :], 0.0)
    combine_map = jnp.sum(weighted.reshape(EXPERTS * MOST, tok_rows, TOP), axis=2)
    mixture = jnp.dot(
        combine_map.T,
        per_expert,
        precision=lax.Precision.HIGHEST,
        preferred_element_type=jnp.float32,
    )
    return (stream + mixture).astype(jnp.bfloat16)


def solution(mesh):
    in_specs = (
        P("dp", "head"),
        P("dp", "head", None),
        P("dp", "head", None),
        P("dp", "head", None),
        P("dp", "head", None, None),
        P("dp", "head", None, None),
        P("dp"),
        P("dp", "head", None),
        P("head", "dp"),
        P("head"),
        P("dp", None),
        P("dp", None),
        P("dp", None, None, "head"),
        P("dp", "head", None),
    )
    out_specs = P("dp", "head")
    return jax.shard_map(shards, mesh=mesh, in_specs=in_specs, out_specs=out_specs, check_vma=False)
```

profile of v0, /device:TPU:0, one launch (start us, length us, event | category | flops | bytes accessed | tf_op | source)
XLA Modules:
  0.0 169.4 jit_solution(6646213300250157299)
XLA Ops:
  6.5 0.0 copy-start
  6.5 0.9 fusion.19
  7.5 0.2 broadcast_in_dim.28
  7.7 0.3 reshape.95
  8.0 0.7 iota_compare_fusion.1
  8.8 0.8 fusion.30
  9.6 3.5 %select_reduce_fusion = (f32[4,2,4]{2,1,0:T(2,128)S(1)}, f32[4,2,4,2048]{3,2,1,0:T(4,128)S(1)}) fusion(pred[4,2,2048]{2,1,0:T(4,128)(4,1)S(1)} %copy.32, bf16[4,2,4,128]{3,2,1,0:T(4,128)(2,1)} %bitcast.52, bf16[4,2,2048,128]{3,2,1,0:T(8,128)(2,1)} %param.18), kind=kOutput, calls=%fused_computation.19 | convolution fusion | flops 16973792 | bytes 4481152 | tf_op jit(solution)/shard_map/bkgd,bksd->bkgs/dot_general | solution.py:48
  13.1 0.3 fusion.20
  13.5 0.7 convert_element_type.55
  14.1 2.9 %fusion.18 = bf16[4,2,4,128]{3,2,1,0:T(4,128)(2,1)S(1)} fusion(bf16[4,2,2048,128]{3,2,1,0:T(8,128)(2,1)} %param.19, f32[4,2,4,2048]{3,2,1,0:T(4,128)S(1)} %get-tuple-element.8, f32[4,2,4]{2,1,0:T(2,128)S(1)} %get-tuple-element.6, f32[4,2,4]{2,1,0:T(2,128)S(1)} %multiply_maximum_fusion, pred[4,2,2048]{2,1,0:T(4,128)(4,1)S(1)} %copy.32, ...), kind=kOutput, calls=%fused_computation.17 | convolution fusion | flops 17051648 | bytes 4485504 | tf_op jit(solution)/shard_map/bkgs,bksd->bkgd/dot_general | solution.py:64
  17.1 32.4 %all-gather = bf16[8,4,1024]{2,1,0:T(4,128)(2,1)S(1)} all-gather(bf16[1,4,1024]{2,1,0:T(4,128)(2,1)S(1)} %reshape.99), channel_id=1, replica_groups=mesh['dp'=8,'head'=4] {'dp'}, dimensions={0}, use_global_device_ids=true | all-gather | bytes 73728 | tf_op jit(solution)/shard_map/all_gather | solution.py:72
  49.5 0.0 copy-done
  49.5 0.3 convolution_convert_fusion.1
  49.7 0.6 all_to_all.20
  50.4 5.5 %all-to-all-start = ((bf16[8,4,512]{2,1,0:T(4,128)(2,1)}), bf16[8,4,512]{2,1,0:T(4,128)(2,1)S(1)}, u32[]{:S(2)}, u32[]{:S(2)}) async-start(bf16[8,4,512]{2,1,0:T(4,128)(2,1)} %all_to_all.20), calls=%async_computation | async-start | bytes 65536 | tf_op jit(solution)/shard_map/all_to_all | solution.py:74
  55.8 0.0 reduce-scatter.7.cloned.1.call-start
  55.9 0.8 copy.33
  56.7 0.1 eq.47
  56.7 0.1 fusion.28
  56.8 0.2 select_reduce_fusion.2
  57.0 0.1 reduce_sum.44
  57.1 0.1 copy.35
  57.2 5.3 %all_gather.11 = f32[4096]{0:T(1024)S(1)} all-gather(f32[1024]{0:T(1024)} %param.23), channel_id=1, replica_groups=mesh['dp'=8,'head'=4] {'head'}, dimensions={0}, use_global_device_ids=true | all-gather | bytes 20480 | tf_op jit(solution)/shard_map/all_gather | solution.py:82
  62.5 0.0 all-to-all-done
  62.6 1.4 copy.40
  64.0 0.0 reduce-scatter.7.cloned.1.call-update
  64.0 0.0 reduce-scatter.5.cloned.1.call-start
  64.0 0.1 fusion.29
  64.1 26.2 %reduce-scatter.7.cloned.1.call-done = bf16[1024,4]{1,0:T(8,128)(2,1)} async-done(((bf16[4096,4]{1,0:T(8,128)(2,1)}), bf16[1024,4]{1,0:T(8,128)(2,1)}) %reduce-scatter.7.cloned.1.call-update) | async-done | bytes 8208
  90.3 1.1 copy.41
  91.4 0.7 convert_add_fusion
  92.1 5.2 %all_gather.10 = f32[4,4096]{1,0:T(4,128)S(1)} all-gather(f32[4,1024]{1,0:T(4,128)S(1)} %convert_add_fusion), channel_id=1, replica_groups=mesh['dp'=8,'head'=4] {'head'}, dimensions={1}, use_global_device_ids=true | all-gather | bytes 81920 | tf_op jit(solution)/shard_map/all_gather | solution.py:81
  97.3 0.1 multiply_reduce_fusion
  97.5 0.3 convolution_convert_fusion
  97.7 0.1 reshape_reshape.3
  97.8 12.8 %all_to_all.29 = bf16[8,2,4096]{2,1,0:T(2,128)(2,1)S(1)} all-to-all(bf16[8,2,4096]{2,1,0:T(2,128)(2,1)S(1)} %reshape_reshape.3), channel_id=1, replica_groups=mesh['dp'=8,'head'=4] {'dp'}, dimensions={0} | all-to-all | bytes 262144 | tf_op jit(solution)/shard_map/all_to_all | solution.py:106
  110.7 0.1 reshape.97
  110.7 6.2 %fusion.4 = f32[16,1792]{1,0:T(8,128)S(1)} fusion(bf16[16,4096]{1,0:T(8,128)(2,1)S(1)} %reshape.97, bf16[1,2,4096,1792]{3,2,1,0:T(8,128)(2,1)} %param.26), kind=kOutput, calls=%fused_computation.4 | convolution fusion | flops 234881024 | bytes 14925824 | tf_op jit(solution)/shard_map/dot_general | solution.py:109
  117.0 0.0 copy-start.2
  117.0 0.0 copy-start.1
  117.0 6.3 %fusion.14 = bf16[16,1792]{1,0:T(8,128)(2,1)S(1)} fusion(bf16[16,4096]{1,0:T(8,128)(2,1)S(1)} %reshape.97, bf16[1,2,4096,1792]{3,2,1,0:T(8,128)(2,1)} %param.26, f32[16,1792]{1,0:T(8,128)S(1)} %fusion.4), kind=kOutput, calls=%fused_computation.12 | convolution fusion | flops 235053056 | bytes 14983168 | tf_op jit(solution)/shard_map/dot_general | solution.py:110
  123.3 7.8 %fusion.8 = bf16[8,2,4096]{2,0,1:T(8,128)(2,1)} fusion(bf16[1,1792,4096]{2,1,0:T(8,128)(2,1)} %param.27, bf16[8,2,1792]{2,1,0:T(2,128)(2,1)S(1)} %dot_general.36), kind=kOutput, calls=%fused_computation.8 | convolution fusion | flops 234946560 | bytes 14868480 | tf_op jit(solution)/shard_map/dot_general | solution.py:112
  131.1 0.0 reduce-scatter.5.cloned.1.call-update
  131.2 17.0 %reduce-scatter.5.cloned.1.call-done = bf16[8,2,1024]{2,0,1:T(8,128)(2,1)} async-done(((bf16[8,2,4096]{2,0,1:T(8,128)(2,1)}), bf16[8,2,1024]{2,0,1:T(8,128)(2,1)}) %reduce-scatter.5.cloned.1.call-update) | async-done | bytes 32784 | tf_op jit(solution)/shard_map/reduce_scatter | solution.py:115
  148.2 1.4 copy.37
  149.6 5.5 %all-to-all-start.2 = ((bf16[8,2,1024]{2,1,0:T(2,128)(2,1)}), bf16[8,2,1024]{2,1,0:T(2,128)(2,1)S(1)}, u32[]{:S(2)}, u32[]{:S(2)}) async-start(bf16[8,2,1024]{2,1,0:T(2,128)(2,1)} %copy.37), calls=%async_computation.3 | async-start | bytes 65536 | tf_op jit(solution)/shard_map/all_to_all | solution.py:118
  155.1 0.0 copy-done.2
  155.1 0.1 select_reduce_fusion.1
  155.2 6.6 %all-to-all-done.2 = bf16[8,2,1024]{2,1,0:T(2,128)(2,1)S(1)} async-done(((bf16[8,2,1024]{2,1,0:T(2,128)(2,1)}), bf16[8,2,1024]{2,1,0:T(2,128)(2,1)S(1)}, u32[]{:S(2)}, u32[]{:S(2)}) %all-to-all-start.2) | async-done | bytes 32800 | tf_op jit(solution)/shard_map/all_to_all | solution.py:118
  161.8 0.0 copy-done.1
  161.8 0.7 fusion.17
  (13 shorter events, 0.2 us)
Async XLA Ops:
  6.5 42.9 %copy-start = (bf16[1024,512]{1,0:T(8,128)(2,1)S(1)}, bf16[1024,512]{1,0:T(8,128)(2,1)}, u32[]{:S(2)}) copy-start(bf16[1024,512]{1,0:T(8,128)(2,1)} %param.22) | copy-start | bytes 3145732
  50.4 12.2 %all-to-all-start = ((bf16[8,4,512]{2,1,0:T(4,128)(2,1)}), bf16[8,4,512]{2,1,0:T(4,128)(2,1)S(1)}, u32[]{:S(2)}, u32[]{:S(2)}) async-start(bf16[8,4,512]{2,1,0:T(4,128)(2,1)} %all_to_all.20), calls=%async_computation | async-start | bytes 65536 | tf_op jit(solution)/shard_map/all_to_all | solution.py:74
  55.8 34.5 %reduce-scatter.7.cloned.1.call-start = ((), (), s32[]{:S(2)}) async-start(), calls=%async_computation.6 | async-start | bytes 1310720
  64.0 84.2 %reduce-scatter.5.cloned.1.call-start = ((), (), s32[]{:S(2)}) async-start(), calls=%async_computation.5 | async-start | bytes 163840 | tf_op jit(solution)/shard_map/reduce_scatter | solution.py:115
  117.0 38.1 %copy-start.2 = (f32[4,2]{0,1:T(2,128)S(1)}, f32[4,2]{0,1:T(2,128)}, u32[]{:S(2)}) copy-start(f32[4,2]{0,1:T(2,128)} %param.25) | copy-start | bytes 100
  117.0 44.8 %copy-start.1 = (bf16[4,1024]{1,0:T(4,128)(2,1)S(1)}, bf16[4,1024]{1,0:T(4,128)(2,1)}, u32[]{:S(2)}) copy-start(bf16[4,1024]{1,0:T(4,128)(2,1)} %param.14) | copy-start | bytes 24580
  149.6 12.2 %all-to-all-start.2 = ((bf16[8,2,1024]{2,1,0:T(2,128)(2,1)}), bf16[8,2,1024]{2,1,0:T(2,128)(2,1)S(1)}, u32[]{:S(2)}, u32[]{:S(2)}) async-start(bf16[8,2,1024]{2,1,0:T(2,128)(2,1)} %copy.37), calls=%async_computation.3 | async-start | bytes 65536 | tf_op jit(solution)/shard_map/all_to_all | solution.py:118
Sparse Core Ops, SparseCore 0:
  64.1 26.1 reduce-scatter.6
  131.3 16.8 reduce-scatter.4
where the time goes:
time: 170 us; the launch traced here: 169 us
  blocking collectives  55.7 us (33%)
  waiting for transfers between devices  49.8 us (29%)
  matrix products  28.9 us (17%)
  between operations  13.6 us (8%)
  starting transfers between devices  11.1 us (7%)
  local copies, waits for them, and re-layouts  6.35 us (4%)
  other arithmetic  4 us (2%)
    all_gather x1, blocking collectives, shards(): every_row = lax.all_gather(attn_rows, 'dp', axis=0, tiled=True)  32.4 us
    unnamed x3, waiting for transfers between devices  26.2 us
    reduce_scatter x1, waiting for transfers between devices, shards(): lax.psum_scatter(slab_out.astype(jnp.bfloat16), 'head', scatter_dimension...  17 us
    all_to_all x1, blocking collectives, shards(): lax.all_to_all(outgoing, 'dp', split_axis=0, concat_axis=0, tiled=True)  12.8 us
    dot_general x1, matrix products, shards(): jnp.dot(hidden, w_down[0], preferred_element_type=jnp.float32)  7.82 us
    all_to_all x1, waiting for transfers between devices, shards(): lax.all_to_all(summed_total.astype(jnp.bfloat16), 'dp', split_axis=0, con...  6.6 us
    dot_general x1, matrix products, shards(): up_act = jnp.dot(flat_rows, w_in[0, 1], preferred_element_type=jnp.float32)  6.3 us
    dot_general x1, matrix products, shards(): jnp.dot(flat_rows, w_in[0, 0], preferred_element_type=jnp.float32)  6.24 us
  transfers between devices with their start and end apart: 4, of which 3 were waited for; matrix products, arithmetic and copies ran while one was open for 1% of the time, Pallas kernels for 0%

commit v1 on v0

--- a/solution.py
+++ b/solution.py
@@ -69,7 +69,14 @@
         + own_weight.astype(jnp.float32)[..., None] * value_new.astype(jnp.float32)[:, :, None, :]
     )
     attn_rows = attended.reshape(tok_rows, head_local * head_dim).astype(jnp.bfloat16)
-    every_row = lax.all_gather(attn_rows, "dp", axis=0, tiled=True)
+    ways, here, step = (lax.axis_size("dp"), lax.axis_index("dp"), attn_rows.shape[0])
+    line, have = (attn_rows, 1)
+    while have < ways:
+        line = jnp.concatenate(
+            [line, lax.ppermute(line, "dp", [(d, (d - have) % ways) for d in range(ways)])], axis=0
+        )
+        have = 2 * have
+    every_row = jnp.roll(line, here * step, axis=0)
     column_part = jnp.dot(every_row, w_out, preferred_element_type=jnp.float32)
     head_partial = lax.all_to_all(
         column_part.astype(jnp.bfloat16), "dp", split_axis=0, concat_axis=1, tiled=True

time: 170 us -> 155 us (0.912)
  blocking collectives: 55.7 us -> 23.3 us
  starting transfers between devices: 11.1 us -> 21.5 us
  waiting for transfers between devices: 49.8 us -> 56.9 us
    all_gather x1 -> x0, blocking collectives: 32.4 us -> none  [shards(): every_row = lax.all_gather(attn_rows, 'dp', axis=0, tiled=True)]
    ppermute x0 -> x3, starting transfers between devices: none -> 7.88 us  [shards(): lax.ppermute(line, 'dp', [(d, (d - have) % ways) for d in range(ways)])]
    ppermute x0 -> x3, waiting for transfers between devices: none -> 7.01 us  [shards(): lax.ppermute(line, 'dp', [(d, (d - have) % ways) for d in range(ways)])]
    all_to_all x1, starting transfers between devices: 5.46 us -> 8.05 us  [shards(): lax.all_to_all(column_part.astype(jnp.bfloat16), 'dp', split_axis=0, conc...]
  transfers between devices with their start and end apart: 4 -> 7, of which waited for: 3 -> 7; matrix products, arithmetic and copies ran while one was open for 1% -> 1% of each run, Pallas kernels for 0% -> 0%
where the time goes in v1:
time: 155 us
  waiting for transfers between devices  56.9 us (37%)
  matrix products  28.8 us (19%)
  blocking collectives  23.3 us (15%)
  starting transfers between devices  21.5 us (14%)
  between operations  13.6 us (9%)
  local copies, waits for them, and re-layouts  6.37 us (4%)
  other arithmetic  4.03 us (3%)
    unnamed x3, waiting for transfers between devices  25 us
    reduce_scatter x1, waiting for transfers between devices, shards(): lax.psum_scatter(slab_out.astype(jnp.bfloat16), 'head', scatter_dimension...  17 us
    all_to_all x1, blocking collectives, shards(): lax.all_to_all(outgoing, 'dp', split_axis=0, concat_axis=0, tiled=True)  12.8 us
    all_to_all x1, starting transfers between devices, shards(): lax.all_to_all(column_part.astype(jnp.bfloat16), 'dp', split_axis=0, conc...  8.05 us
    ppermute x3, starting transfers between devices, shards(): lax.ppermute(line, 'dp', [(d, (d - have) % ways) for d in range(ways)])  7.88 us
    dot_general x1, matrix products, shards(): jnp.dot(hidden, w_down[0], preferred_element_type=jnp.float32)  7.82 us
    ppermute x3, waiting for transfers between devices, shards(): lax.ppermute(line, 'dp', [(d, (d - have) % ways) for d in range(ways)])  7.01 us
    all_to_all x1, waiting for transfers between devices, shards(): lax.all_to_all(summed_total.astype(jnp.bfloat16), 'dp', split_axis=0, con...  6.6 us
  transfers between devices with their start and end apart: 7, of which 7 were waited for; matrix products, arithmetic and copies ran while one was open for 1% of the time, Pallas kernels for 0%

profile of v1, /device:TPU:0, one launch (start us, length us, event | category | flops | bytes accessed | tf_op | source)
XLA Modules:
  0.0 154.5 jit_solution(14329255363334622928)
XLA Ops:
  6.5 0.0 copy-start
  6.5 0.9 fusion.19
  7.5 0.2 broadcast_in_dim.28
  7.7 0.3 reshape.95
  8.0 0.7 iota_compare_fusion.1
  8.8 0.8 fusion.31
  9.6 3.5 %select_reduce_fusion = (f32[4,2,4]{2,1,0:T(2,128)S(1)}, f32[4,2,4,2048]{3,2,1,0:T(4,128)S(1)}) fusion(pred[4,2,2048]{2,1,0:T(4,128)(4,1)S(1)} %copy.32, bf16[4,2,4,128]{3,2,1,0:T(4,128)(2,1)} %bitcast.51, bf16[4,2,2048,128]{3,2,1,0:T(8,128)(2,1)} %param.18), kind=kOutput, calls=%fused_computation.19 | convolution fusion | flops 16973792 | bytes 4481152 | tf_op jit(solution)/shard_map/bkgd,bksd->bkgs/dot_general | solution.py:48
  13.1 0.3 fusion.20
  13.5 0.7 convert_element_type.55
  14.1 2.9 %fusion.18 = bf16[4,2,4,128]{3,2,1,0:T(4,128)(2,1)S(1)} fusion(bf16[4,2,2048,128]{3,2,1,0:T(8,128)(2,1)} %param.19, f32[4,2,4,2048]{3,2,1,0:T(4,128)S(1)} %get-tuple-element.8, f32[4,2,4]{2,1,0:T(2,128)S(1)} %get-tuple-element.6, f32[4,2,4]{2,1,0:T(2,128)S(1)} %multiply_maximum_fusion, pred[4,2,2048]{2,1,0:T(4,128)(4,1)S(1)} %copy.32, ...), kind=kOutput, calls=%fused_computation.17 | convolution fusion | flops 17051648 | bytes 4485504 | tf_op jit(solution)/shard_map/bkgs,bksd->bkgd/dot_general | solution.py:64
  17.1 6.1 %collective-permute-start = (bf16[4,1024]{1,0:T(4,128)(2,1)S(1)}, bf16[4,1024]{1,0:T(4,128)(2,1)S(1)}, u32[]{:S(2)}, u32[]{:S(2)}) collective-permute-start(bf16[4,1024]{1,0:T(4,128)(2,1)S(1)} %convert_element_type.57), channel_id=1, source_target_pairs={{0,28},{4,0},{8,4},{12,8},{16,12},{20,16},{24,20},{28,24},{1,29},{... | collective-permute-start | bytes 24584 | tf_op jit(solution)/shard_map/ppermute | solution.py:76
  23.1 0.8 copy.33
  23.9 0.1 eq.50
  24.0 0.5 collective-permute-done
  24.5 1.4 collective-permute-start.1
  25.9 0.1 fusion.29
  26.0 2.3 %collective-permute-done.1 = bf16[8,1024]{1,0:T(8,128)(2,1)S(1)} collective-permute-done((bf16[8,1024]{1,0:T(8,128)(2,1)S(1)}, bf16[8,1024]{1,0:T(8,128)(2,1)S(1)}, u32[]{:S(2)}, u32[]{:S(2)}) %collective-permute-start.1) | collective-permute-done | bytes 16416 | tf_op jit(solution)/shard_map/ppermute | solution.py:76
  28.3 0.4 collective-permute-start.2
  28.8 0.2 select_reduce_fusion.2
  28.9 0.1 reduce_sum.44
  29.0 4.2 %collective-permute-done.2 = bf16[16,1024]{1,0:T(8,128)(2,1)S(1)} collective-permute-done((bf16[16,1024]{1,0:T(8,128)(2,1)S(1)}, bf16[16,1024]{1,0:T(8,128)(2,1)S(1)}, u32[]{:S(2)}, u32[]{:S(2)}) %collective-permute-start.2) | collective-permute-done | bytes 32800 | tf_op jit(solution)/shard_map/ppermute | solution.py:76
  33.2 0.1 concatenate.16
  33.3 0.0 copy-done
  33.3 0.3 convolution_convert_fusion.1
  33.6 0.6 all_to_all.20
  34.2 8.0 %all-to-all-start = ((bf16[8,4,512]{2,1,0:T(4,128)(2,1)}), bf16[8,4,512]{2,1,0:T(4,128)(2,1)S(1)}, u32[]{:S(2)}, u32[]{:S(2)}) async-start(bf16[8,4,512]{2,1,0:T(4,128)(2,1)} %all_to_all.20), calls=%async_computation | async-start | bytes 65536 | tf_op jit(solution)/shard_map/all_to_all | solution.py:81
  42.2 0.0 reduce-scatter.7.cloned.1.call-start
  42.3 0.1 copy.35
  42.4 5.3 %all_gather.7 = f32[4096]{0:T(1024)S(1)} all-gather(f32[1024]{0:T(1024)} %param.23), channel_id=1, replica_groups=mesh['dp'=8,'head'=4] {'head'}, dimensions={0}, use_global_device_ids=true | all-gather | bytes 20480 | tf_op jit(solution)/shard_map/all_gather | solution.py:89
  47.7 1.2 all-to-all-done
  48.9 1.4 copy.40
  50.3 0.0 reduce-scatter.7.cloned.1.call-update
  50.4 0.0 reduce-scatter.5.cloned.1.call-start
  50.4 0.1 fusion.30
  50.5 25.0 %reduce-scatter.7.cloned.1.call-done = bf16[1024,4]{1,0:T(8,128)(2,1)} async-done(((bf16[4096,4]{1,0:T(8,128)(2,1)}), bf16[1024,4]{1,0:T(8,128)(2,1)}) %reduce-scatter.7.cloned.1.call-update) | async-done | bytes 8208
  75.5 1.1 copy.41
  76.5 0.7 convert_add_fusion
  77.3 5.2 %all_gather.6 = f32[4,4096]{1,0:T(4,128)S(1)} all-gather(f32[4,1024]{1,0:T(4,128)S(1)} %convert_add_fusion), channel_id=1, replica_groups=mesh['dp'=8,'head'=4] {'head'}, dimensions={1}, use_global_device_ids=true | all-gather | bytes 81920 | tf_op jit(solution)/shard_map/all_gather | solution.py:88
  82.5 0.1 multiply_reduce_fusion
  82.6 0.3 convolution_convert_fusion
  82.9 0.1 reshape_reshape.3
  83.0 12.8 %all_to_all.29 = bf16[8,2,4096]{2,1,0:T(2,128)(2,1)S(1)} all-to-all(bf16[8,2,4096]{2,1,0:T(2,128)(2,1)S(1)} %reshape_reshape.3), channel_id=1, replica_groups=mesh['dp'=8,'head'=4] {'dp'}, dimensions={0} | all-to-all | bytes 262144 | tf_op jit(solution)/shard_map/all_to_all | solution.py:113
  95.8 0.1 reshape.97
  95.8 6.2 %fusion.4 = f32[16,1792]{1,0:T(8,128)S(1)} fusion(bf16[16,4096]{1,0:T(8,128)(2,1)S(1)} %reshape.97, bf16[1,2,4096,1792]{3,2,1,0:T(8,128)(2,1)} %param.26), kind=kOutput, calls=%fused_computation.4 | convolution fusion | flops 234881024 | bytes 14925824 | tf_op jit(solution)/shard_map/dot_general | solution.py:116
  102.1 0.0 copy-start.2
  102.1 0.0 copy-start.1
  102.1 6.3 %fusion.14 = bf16[16,1792]{1,0:T(8,128)(2,1)S(1)} fusion(bf16[16,4096]{1,0:T(8,128)(2,1)S(1)} %reshape.97, bf16[1,2,4096,1792]{3,2,1,0:T(8,128)(2,1)} %param.26, f32[16,1792]{1,0:T(8,128)S(1)} %fusion.4), kind=kOutput, calls=%fused_computation.12 | convolution fusion | flops 235053056 | bytes 14983168 | tf_op jit(solution)/shard_map/dot_general | solution.py:117
  108.5 7.8 %fusion.8 = bf16[8,2,4096]{2,0,1:T(8,128)(2,1)} fusion(bf16[1,1792,4096]{2,1,0:T(8,128)(2,1)} %param.27, bf16[8,2,1792]{2,1,0:T(2,128)(2,1)S(1)} %dot_general.36), kind=kOutput, calls=%fused_computation.8 | convolution fusion | flops 234946560 | bytes 14868480 | tf_op jit(solution)/shard_map/dot_general | solution.py:119
  116.3 0.0 reduce-scatter.5.cloned.1.call-update
  116.3 17.0 %reduce-scatter.5.cloned.1.call-done = bf16[8,2,1024]{2,0,1:T(8,128)(2,1)} async-done(((bf16[8,2,4096]{2,0,1:T(8,128)(2,1)}), bf16[8,2,1024]{2,0,1:T(8,128)(2,1)}) %reduce-scatter.5.cloned.1.call-update) | async-done | bytes 32784 | tf_op jit(solution)/shard_map/reduce_scatter | solution.py:122
  133.3 1.4 copy.37
  134.7 5.5 %all-to-all-start.2 = ((bf16[8,2,1024]{2,1,0:T(2,128)(2,1)}), bf16[8,2,1024]{2,1,0:T(2,128)(2,1)S(1)}, u32[]{:S(2)}, u32[]{:S(2)}) async-start(bf16[8,2,1024]{2,1,0:T(2,128)(2,1)} %copy.37), calls=%async_computation.3 | async-start | bytes 65536 | tf_op jit(solution)/shard_map/all_to_all | solution.py:125
  140.2 0.0 copy-done.2
  140.2 0.1 select_reduce_fusion.1
  140.3 6.6 %all-to-all-done.2 = bf16[8,2,1024]{2,1,0:T(2,128)(2,1)S(1)} async-done(((bf16[8,2,1024]{2,1,0:T(2,128)(2,1)}), bf16[8,2,1024]{2,1,0:T(2,128)(2,1)S(1)}, u32[]{:S(2)}, u32[]{:S(2)}) %all-to-all-start.2) | async-done | bytes 32800 | tf_op jit(solution)/shard_map/all_to_all | solution.py:125
  146.9 0.0 copy-done.1
  147.0 0.7 fusion.17
  (14 shorter events, 0.2 us)
Async XLA Ops:
  6.5 26.8 %copy-start = (bf16[1024,512]{1,0:T(8,128)(2,1)S(1)}, bf16[1024,512]{1,0:T(8,128)(2,1)}, u32[]{:S(2)}) copy-start(bf16[1024,512]{1,0:T(8,128)(2,1)} %param.22) | copy-start | bytes 3145732
  17.1 7.4 %collective-permute-start = (bf16[4,1024]{1,0:T(4,128)(2,1)S(1)}, bf16[4,1024]{1,0:T(4,128)(2,1)S(1)}, u32[]{:S(2)}, u32[]{:S(2)}) collective-permute-start(bf16[4,1024]{1,0:T(4,128)(2,1)S(1)} %convert_element_type.57), channel_id=1, source_target_pairs={{0,28},{4,0},{8,4},{12,8},{16,12},{20,16},{24,20},{28,24},{1,29},{... | collective-permute-start | bytes 24584 | tf_op jit(solution)/shard_map/ppermute | solution.py:76
  24.5 3.8 %collective-permute-start.1 = (bf16[8,1024]{1,0:T(8,128)(2,1)S(1)}, bf16[8,1024]{1,0:T(8,128)(2,1)S(1)}, u32[]{:S(2)}, u32[]{:S(2)}) collective-permute-start(bf16[8,1024]{1,0:T(8,128)(2,1)S(1)} %pad_maximum_fusion.1), channel_id=1, source_target_pairs={{0,24},{4,28},{8,0},{12,4},{16,8},{20,12},{24,16},{28,20},{1,25},{... | collective-permute-start | bytes 49160 | tf_op jit(solution)/shard_map/ppermute | solution.py:76
  28.3 4.9 %collective-permute-start.2 = (bf16[16,1024]{1,0:T(8,128)(2,1)S(1)}, bf16[16,1024]{1,0:T(8,128)(2,1)S(1)}, u32[]{:S(2)}, u32[]{:S(2)}) collective-permute-start(bf16[16,1024]{1,0:T(8,128)(2,1)S(1)} %pad_maximum_fusion), channel_id=1, source_target_pairs={{0,16},{4,20},{8,24},{12,28},{16,0},{20,4},{24,8},{28,12},{1,17},{... | collective-permute-start | bytes 98312 | tf_op jit(solution)/shard_map/ppermute | solution.py:76
  34.2 14.7 %all-to-all-start = ((bf16[8,4,512]{2,1,0:T(4,128)(2,1)}), bf16[8,4,512]{2,1,0:T(4,128)(2,1)S(1)}, u32[]{:S(2)}, u32[]{:S(2)}) async-start(bf16[8,4,512]{2,1,0:T(4,128)(2,1)} %all_to_all.20), calls=%async_computation | async-start | bytes 65536 | tf_op jit(solution)/shard_map/all_to_all | solution.py:81
  42.2 33.2 %reduce-scatter.7.cloned.1.call-start = ((), (), s32[]{:S(2)}) async-start(), calls=%async_computation.6 | async-start | bytes 1310720
  50.4 83.0 %reduce-scatter.5.cloned.1.call-start = ((), (), s32[]{:S(2)}) async-start(), calls=%async_computation.5 | async-start | bytes 163840 | tf_op jit(solution)/shard_map/reduce_scatter | solution.py:122
  102.1 38.1 %copy-start.2 = (f32[4,2]{0,1:T(2,128)S(1)}, f32[4,2]{0,1:T(2,128)}, u32[]{:S(2)}) copy-start(f32[4,2]{0,1:T(2,128)} %param.25) | copy-start | bytes 100
  102.1 44.8 %copy-start.1 = (bf16[4,1024]{1,0:T(4,128)(2,1)S(1)}, bf16[4,1024]{1,0:T(4,128)(2,1)}, u32[]{:S(2)}) copy-start(bf16[4,1024]{1,0:T(4,128)(2,1)} %param.14) | copy-start | bytes 24580
  134.7 12.2 %all-to-all-start.2 = ((bf16[8,2,1024]{2,1,0:T(2,128)(2,1)}), bf16[8,2,1024]{2,1,0:T(2,128)(2,1)S(1)}, u32[]{:S(2)}, u32[]{:S(2)}) async-start(bf16[8,2,1024]{2,1,0:T(2,128)(2,1)} %copy.37), calls=%async_computation.3 | async-start | bytes 65536 | tf_op jit(solution)/shard_map/all_to_all | solution.py:125
Sparse Core Ops, SparseCore 0:
  50.5 24.9 reduce-scatter.6
  116.4 16.8 reduce-scatter.4
